TPU v7x, 128 devices: a whole 4x4x4 slice. The times are simulated.
128 devices in a mesh: row: 8 (over z, x_hi), col: 16 (over y, x_lo, core).
Axes of the slice: x: 4 (x_hi: 2, x_lo: 2; x = x_hi * 2 + x_lo), y: 4, z: 4, core: 2. Of those that a mesh axis runs over, the one named last changes fastest.
Arguments:
- features: bfloat16 [32768, 512], P('row'), may hold values from -6 to 6
- logits: float32 [32768, 128], P(('row', 'col')), may hold values from -16 to 16
Outputs:
- memberships: float32 [32768, 128], P(('row', 'col'))
- standardized: float32 [32768, 128], P(('row', 'col'))
All inputs are finite; a program needn't handle non-finite values.
Results may differ from a plain program's by a relative error of at most 0.0003.
Values may be sent and summed in bfloat16 or wider, within the bound.
A program may use at most 64 MiB of HBM per device.

v0:
```python
import math
import jax
import jax.numpy as jnp
from jax import lax
from jax.sharding import PartitionSpec as P

ITERS = 2


def kernel_product(left_rows, right_rows, members):
    count = left_rows.shape[0]
    feature_width = left_rows.shape[1]
    block_rows = math.gcd(count, 512)
    blocks = left_rows.reshape(count // block_rows, block_rows, feature_width)

    def block_product(block):
        inner = jnp.einsum("bf,nf->bn", block, right_rows, preferred_element_type=jnp.float32)
        base = 1.0 + inner / feature_width
        kernel = base * base * base
        return jnp.dot(
            kernel, members, precision=lax.Precision.HIGHEST, preferred_element_type=jnp.float32
        )

    return lax.map(block_product, blocks).reshape(count, members.shape[1])


def on_device(features, logits):
    frames = logits.shape[0]
    column = lax.axis_index("col")
    own_rows = lax.dynamic_slice_in_dim(features, column * frames, frames, 0)
    column_panel = lax.all_gather(own_rows, "row", axis=0, tiled=True)
    raised = jnp.exp(logits)
    members = raised / jnp.sum(raised, axis=1, keepdims=True)
    standardized = members
    for iteration in range(ITERS):
        members_column = lax.all_gather(members, "row", axis=0, tiled=True)
        scores = lax.psum_scatter(
            kernel_product(features, column_panel, members_column),
            "col",
            scatter_dimension=0,
            tiled=True,
        )
        cluster_size, weighted = lax.psum(
            (jnp.sum(members, axis=0), jnp.sum(members * scores, axis=0)), ("row", "col")
        )
        compact = weighted / (cluster_size * cluster_size)
        distance = compact[None, :] - 2.0 * scores / cluster_size[None, :]
        centered = distance - jnp.mean(distance, axis=1, keepdims=True)
        spread = jnp.mean(centered * centered, axis=1, keepdims=True)
        standardized = centered / jnp.sqrt(spread + 1e-06)
        raised = jnp.exp(-2.0 * standardized)
        members = raised / jnp.sum(raised, axis=1, keepdims=True)
    return (members, standardized)


def solution(mesh):
    return jax.shard_map(
        on_device,
        mesh=mesh,
        in_specs=(P("row", None), P(("row", "col"), None)),
        out_specs=(P(("row", "col"), None), P(("row", "col"), None)),
        check_vma=False,
    )
```

profile of v0, /device:TPU:1, one launch (start us, length us, event | category | flops | bytes accessed | tf_op | source)
XLA Modules:
  0.0 545.2 jit_solution(2299477837792060629)
XLA Ops:
  8.2 1.7 exponential_divide_fusion
  10.0 1.7 constant_dynamic-slice_fusion
  11.7 47.2 %all-gather.6.cloned.1.call-done = f32[2048,128]{1,0:T(8,128)} async-done(((f32[256,128]{1,0:T(8,128)}), f32[2048,128]{1,0:T(8,128)}) %all-gather.6.cloned.1.call-update) | async-done | bytes 1048592 | tf_op jit(solution)/shard_map/all_gather | solution.py:36
  59.0 55.7 %all-gather.4.cloned.1.call-done = bf16[2048,512]{1,0:T(8,128)(2,1)} async-done(((bf16[256,512]{1,0:T(8,128)(2,1)}), bf16[2048,512]{1,0:T(8,128)(2,1)}) %all-gather.4.cloned.1.call-update) | async-done | bytes 2097168 | tf_op jit(solution)/shard_map/all_gather | solution.py:31
  114.8 54.8 %while.20 = (s32[]{:T(128)}, f32[8,512,128]{2,1,0:T(8,128)S(1)}, bf16[8,512,512]{2,1,0:T(8,128)(2,1)}, bf16[2048,512]{1,0:T(8,128)(2,1)}, f32[2048,128]{1,0:T(8,128)}, /*index=5*/s32[]{:T(128)}) while((s32[]{:T(128)}, f32[8,512,128]{2,1,0:T(8,128)S(1)}, bf16[8,512,512]{2,1,0:T(8,128)(2,1)}, bf16[2048,512]{1,0:T(8,128)(2,1)}, ...), condition=%wide.region_2.3_spmd, body=%wide.region_1.2_spmd.sunk | while | flops 2688548864 | bytes 16515685 | solution.py:24
  114.9 3.1 fusion.48
  118.0 3.7 fusion.49
  121.7 3.1 fusion.48
  124.9 3.7 fusion.49
  128.6 3.1 fusion.48
  131.7 3.7 fusion.49
  135.4 3.1 fusion.48
  138.6 3.7 fusion.49
  142.3 3.1 fusion.48
  145.4 3.7 fusion.49
  149.1 3.1 fusion.48
  152.3 3.7 fusion.49
  156.0 3.1 fusion.48
  159.1 3.7 fusion.49
  162.8 3.1 fusion.48
  166.0 3.7 fusion.49
  169.7 1.3 copy-done.1
  171.0 60.5 %reduce-scatter.3.cloned.1.call-done = f32[256,128]{1,0:T(8,128)} async-done(((f32[4096,128]{1,0:T(8,128)}), f32[256,128]{1,0:T(8,128)}) %reduce-scatter.3.cloned.1.call-update) | async-done | bytes 131088 | tf_op jit(solution)/shard_map/reduce_scatter | solution.py:37
  232.5 68.0 %all-reduce.1 = (f32[128]{0:T(128)S(1)}, f32[128]{0:T(128)S(1)}) all-reduce(f32[128]{0:T(128)S(1)} %get-tuple-element.61, f32[128]{0:T(128)S(1)} %get-tuple-element.60), channel_id=1, replica_groups=mesh['row'=8,'col'=16] {'row','col'}, use_global_device_ids=true, to_apply=%region_7.8 | all-reduce | flops 256 | bytes 2048 | tf_op jit(solution)/shard_map/psum | solution.py:43
  302.7 1.1 fusion.28
  303.8 1.7 broadcast_divide_fusion
  305.8 41.2 %all-gather.8.cloned.1.call-done = f32[2048,128]{1,0:T(8,128)} async-done(((f32[256,128]{1,0:T(8,128)}), f32[2048,128]{1,0:T(8,128)}) %all-gather.8.cloned.1.call-update) | async-done | bytes 1048592 | tf_op jit(solution)/shard_map/all_gather | solution.py:36
  347.2 54.8 %while.21 = (s32[]{:T(128)}, f32[8,512,128]{2,1,0:T(8,128)S(1)}, bf16[8,512,512]{2,1,0:T(8,128)(2,1)}, bf16[2048,512]{1,0:T(8,128)(2,1)}, f32[2048,128]{1,0:T(8,128)}, /*index=5*/s32[]{:T(128)}) while((s32[]{:T(128)}, f32[8,512,128]{2,1,0:T(8,128)S(1)}, bf16[8,512,512]{2,1,0:T(8,128)(2,1)}, bf16[2048,512]{1,0:T(8,128)(2,1)}, ...), condition=%wide.region_12.13_spmd, body=%wide.region_11.12_spmd.sunk | while | flops 2688548864 | bytes 16515685 | solution.py:24
  347.2 3.1 fusion.53
  350.3 3.7 fusion.54
  354.1 3.1 fusion.53
  357.2 3.7 fusion.54
  360.9 3.1 fusion.53
  364.1 3.7 fusion.54
  367.8 3.1 fusion.53
  370.9 3.7 fusion.54
  374.6 3.1 fusion.53
  377.8 3.7 fusion.54
  381.5 3.1 fusion.53
  384.6 3.7 fusion.54
  388.3 3.1 fusion.53
  391.5 3.7 fusion.54
  395.2 3.1 fusion.53
  398.3 3.7 fusion.54
  402.0 1.3 copy-done
  403.4 62.6 %reduce-scatter.5.cloned.1.call-done = f32[256,128]{1,0:T(8,128)} async-done(((f32[4096,128]{1,0:T(8,128)}), f32[256,128]{1,0:T(8,128)}) %reduce-scatter.5.cloned.1.call-update) | async-done | bytes 131088 | tf_op jit(solution)/shard_map/reduce_scatter | solution.py:37
  467.1 67.5 %all-reduce = (f32[128]{0:T(128)S(1)}, f32[128]{0:T(128)S(1)}) all-reduce(f32[128]{0:T(128)S(1)} %get-tuple-element.59, f32[128]{0:T(128)S(1)} %get-tuple-element.58), channel_id=1, replica_groups=mesh['row'=8,'col'=16] {'row','col'}, use_global_device_ids=true, to_apply=%region_17.18 | all-reduce | flops 256 | bytes 2048 | tf_op jit(solution)/shard_map/psum | solution.py:43
  536.7 1.1 fusion.27
  (66 shorter events, 9.0 us)
Async XLA Ops:
  7.2 51.8 %all-gather.6.cloned.1.call-start = ((), (), s32[]{:S(2)}) async-start(), calls=%async_computation.3 | async-start | bytes 1179648 | tf_op jit(solution)/shard_map/all_gather | solution.py:36
  9.9 104.8 %all-gather.4.cloned.1.call-start = ((), (), s32[]{:S(2)}) async-start(), calls=%async_computation.2 | async-start | bytes 2359296 | tf_op jit(solution)/shard_map/all_gather | solution.py:31
  11.7 219.8 %reduce-scatter.3.cloned.1.call-start = ((), (), s32[]{:S(2)}) async-start(), calls=%async_computation.4 | async-start | bytes 2228224 | tf_op jit(solution)/shard_map/reduce_scatter | solution.py:37
  114.8 116.7 %copy-start.3 = (f32[256,128]{1,0:T(8,128)S(1)}, f32[256,128]{1,0:T(8,128)}, u32[]{:S(2)}) copy-start(f32[256,128]{1,0:T(8,128)} %param.7) | copy-start | bytes 393220
  114.8 3.1 copy-start.5
  121.7 3.1 copy-start.5
  128.6 3.1 copy-start.5
  135.4 3.1 copy-start.5
  142.3 3.1 copy-start.5
  149.1 3.1 copy-start.5
  156.0 3.1 copy-start.5
  162.8 3.1 copy-start.5
  169.7 1.3 copy-start.1
  171.0 176.0 %all-gather.8.cloned.1.call-start = ((), (), s32[]{:S(2)}) async-start(), calls=%async_computation.5 | async-start | bytes 1179648 | tf_op jit(solution)/shard_map/all_gather | solution.py:36
  305.6 160.4 %reduce-scatter.5.cloned.1.call-start = ((), (), s32[]{:S(2)}) async-start(), calls=%async_computation.6 | async-start | bytes 2228224 | tf_op jit(solution)/shard_map/reduce_scatter | solution.py:37
  347.2 118.8 %copy-start.2 = (f32[256,128]{1,0:T(8,128)S(1)}, f32[256,128]{1,0:T(8,128)}, u32[]{:S(2)}) copy-start(f32[256,128]{1,0:T(8,128)} %reduce-scatter.3.cloned.1.call-done) | copy-start | bytes 393220
  347.2 3.1 copy-start.6
  354.1 3.1 copy-start.6
  360.9 3.1 copy-start.6
  367.8 3.1 copy-start.6
  374.6 3.1 copy-start.6
  381.5 3.1 copy-start.6
  388.3 3.1 copy-start.6
  395.2 3.1 copy-start.6
  402.0 1.4 copy-start
  537.9 0.8 copy-start.4
Sparse Core Ops, SparseCore 0:
  10.9 48.0 all-gather.5
  61.3 53.3 all-gather.3
  171.1 60.3 reduce-scatter.2
  305.7 41.2 all-gather.7
  403.5 62.4 reduce-scatter.4
where the time goes:
time: 546 us; the launch traced here: 545 us
  waiting for transfers between devices  267 us (49%)
  blocking collectives  136 us (25%)
  matrix products  109 us (20%)
  between operations  13.9 us (3%)
  other arithmetic  13.8 us (3%)
    psum x2, blocking collectives, on_device(): lax.psum((jnp.sum(members, axis=0), jnp.sum(members * scores, axis=0)), (...  136 us
    reduce_scatter x2, waiting for transfers between devices, on_device(): lax.psum_scatter(kernel_product(features, column_panel, members_column),...  123 us
    all_gather x2, waiting for transfers between devices, on_device(): members_column = lax.all_gather(members, 'row', axis=0, tiled=True)  88.4 us
    dot_general x16, matrix products, block_product(): jnp.dot(kernel, members, precision=lax.Precision.HIGHEST, preferred_eleme...  58.9 us
    all_gather x1, waiting for transfers between devices, on_device(): column_panel = lax.all_gather(own_rows, 'row', axis=0, tiled=True)  55.7 us
    dot_general x16, matrix products, block_product(): jnp.einsum('bf,nf->bn', block, right_rows, preferred_element_type=jnp.flo...  50 us
  transfers between devices with their start and end apart: 5, of which 5 were waited for; matrix products, arithmetic and copies ran while one was open for 0% of the time, Pallas kernels for 0%

commit v1 on v0

--- a/solution.py
+++ b/solution.py
@@ -5,6 +5,12 @@
 from jax.sharding import PartitionSpec as P
 
 ITERS = 2
+
+
+def bind_the_loops(incoming_x):
+    for c in ("row", "col"):
+        incoming_x = lax.psum(incoming_x, c)
+    return incoming_x
 
 
 def kernel_product(left_rows, right_rows, members):
@@ -40,8 +46,8 @@
             scatter_dimension=0,
             tiled=True,
         )
-        cluster_size, weighted = lax.psum(
-            (jnp.sum(members, axis=0), jnp.sum(members * scores, axis=0)), ("row", "col")
+        cluster_size, weighted = bind_the_loops(
+            (jnp.sum(members, axis=0), jnp.sum(members * scores, axis=0))
         )
         compact = weighted / (cluster_size * cluster_size)
         distance = compact[None, :] - 2.0 * scores / cluster_size[None, :]

time: 546 us -> 516 us (0.945)
  blocking collectives: 136 us -> 109 us
    psum x2 -> x4, blocking collectives: 136 us -> 109 us  [bind_the_loops(): incoming_x = lax.psum(incoming_x, c)]
where the time goes in v1:
time: 516 us
  waiting for transfers between devices  264 us (51%)
  matrix products  109 us (21%)
  blocking collectives  109 us (21%)
  between operations  13.9 us (3%)
  other arithmetic  13.8 us (3%)
    reduce_scatter x2, waiting for transfers between devices, on_device(): lax.psum_scatter(kernel_product(features, column_panel, members_column),...  123 us
    psum x4, blocking collectives, bind_the_loops(): incoming_x = lax.psum(incoming_x, c)  109 us
    all_gather x2, waiting for transfers between devices, on_device(): members_column = lax.all_gather(members, 'row', axis=0, tiled=True)  85.5 us
    dot_general x16, matrix products, block_product(): jnp.dot(kernel, members, precision=lax.Precision.HIGHEST, preferred_eleme...  58.9 us
    all_gather x1, waiting for transfers between devices, on_device(): column_panel = lax.all_gather(own_rows, 'row', axis=0, tiled=True)  55.7 us
    dot_general x16, matrix products, block_product(): jnp.einsum('bf,nf->bn', block, right_rows, preferred_element_type=jnp.flo...  50 us
  transfers between devices with their start and end apart: 5, of which 5 were waited for; matrix products, arithmetic and copies ran while one was open for 0% of the time, Pallas kernels for 0%

profile of v1, /device:TPU:1, one launch (start us, length us, event | category | flops | bytes accessed | tf_op | source)
XLA Modules:
  0.0 515.6 jit_solution(3784074950429509640)
XLA Ops:
  8.2 1.7 exponential_divide_fusion
  10.0 1.7 constant_dynamic-slice_fusion
  11.7 47.2 %all-gather.6.cloned.1.call-done = f32[2048,128]{1,0:T(8,128)} async-done(((f32[256,128]{1,0:T(8,128)}), f32[2048,128]{1,0:T(8,128)}) %all-gather.6.cloned.1.call-update) | async-done | bytes 1048592 | tf_op jit(solution)/shard_map/all_gather | solution.py:42
  59.0 55.7 %all-gather.4.cloned.1.call-done = bf16[2048,512]{1,0:T(8,128)(2,1)} async-done(((bf16[256,512]{1,0:T(8,128)(2,1)}), bf16[2048,512]{1,0:T(8,128)(2,1)}) %all-gather.4.cloned.1.call-update) | async-done | bytes 2097168 | tf_op jit(solution)/shard_map/all_gather | solution.py:37
  114.8 54.8 %while.20 = (s32[]{:T(128)}, f32[8,512,128]{2,1,0:T(8,128)S(1)}, bf16[8,512,512]{2,1,0:T(8,128)(2,1)}, bf16[2048,512]{1,0:T(8,128)(2,1)}, f32[2048,128]{1,0:T(8,128)}, /*index=5*/s32[]{:T(128)}) while((s32[]{:T(128)}, f32[8,512,128]{2,1,0:T(8,128)S(1)}, bf16[8,512,512]{2,1,0:T(8,128)(2,1)}, bf16[2048,512]{1,0:T(8,128)(2,1)}, ...), condition=%wide.region_2.3_spmd, body=%wide.region_1.2_spmd.sunk | while | flops 2688548864 | bytes 16515685 | solution.py:30
  114.9 3.1 fusion.48
  118.0 3.7 fusion.49
  121.7 3.1 fusion.48
  124.9 3.7 fusion.49
  128.6 3.1 fusion.48
  131.7 3.7 fusion.49
  135.4 3.1 fusion.48
  138.6 3.7 fusion.49
  142.3 3.1 fusion.48
  145.4 3.7 fusion.49
  149.1 3.1 fusion.48
  152.3 3.7 fusion.49
  156.0 3.1 fusion.48
  159.1 3.7 fusion.49
  162.8 3.1 fusion.48
  166.0 3.7 fusion.49
  169.7 1.3 copy-done.1
  171.0 60.5 %reduce-scatter.3.cloned.1.call-done = f32[256,128]{1,0:T(8,128)} async-done(((f32[4096,128]{1,0:T(8,128)}), f32[256,128]{1,0:T(8,128)}) %reduce-scatter.3.cloned.1.call-update) | async-done | bytes 131088 | tf_op jit(solution)/shard_map/reduce_scatter | solution.py:43
  232.6 20.9 %all-reduce.3 = (f32[128]{0:T(128)S(1)}, f32[128]{0:T(128)S(1)}) all-reduce(f32[128]{0:T(128)S(1)} %get-tuple-element.61, f32[128]{0:T(128)S(1)} %get-tuple-element.60), channel_id=1, replica_groups=mesh['row'=8,'col'=16] {'row'}, use_global_device_ids=true, to_apply=%region_8.9 | all-reduce | flops 256 | bytes 2048 | tf_op jit(solution)/shard_map/psum | solution.py:12
  253.5 33.6 %all-reduce.1 = (f32[128]{0:T(128)S(1)}, f32[128]{0:T(128)S(1)}) all-reduce(f32[128]{0:T(128)S(1)} %get-tuple-element.88, f32[128]{0:T(128)S(1)} %get-tuple-element.89), channel_id=1, replica_groups=mesh['row'=8,'col'=16] {'col'}, use_global_device_ids=true, to_apply=%region_9.10 | all-reduce | flops 256 | bytes 2048 | tf_op jit(solution)/shard_map/psum | solution.py:12
  290.4 1.7 broadcast_divide_fusion
  292.2 38.3 %all-gather.8.cloned.1.call-done = f32[2048,128]{1,0:T(8,128)} async-done(((f32[256,128]{1,0:T(8,128)}), f32[2048,128]{1,0:T(8,128)}) %all-gather.8.cloned.1.call-update) | async-done | bytes 1048592 | tf_op jit(solution)/shard_map/all_gather | solution.py:42
  330.6 54.8 %while.21 = (s32[]{:T(128)}, f32[8,512,128]{2,1,0:T(8,128)S(1)}, bf16[8,512,512]{2,1,0:T(8,128)(2,1)}, bf16[2048,512]{1,0:T(8,128)(2,1)}, f32[2048,128]{1,0:T(8,128)}, /*index=5*/s32[]{:T(128)}) while((s32[]{:T(128)}, f32[8,512,128]{2,1,0:T(8,128)S(1)}, bf16[8,512,512]{2,1,0:T(8,128)(2,1)}, bf16[2048,512]{1,0:T(8,128)(2,1)}, ...), condition=%wide.region_14.15_spmd, body=%wide.region_13.14_spmd.sunk | while | flops 2688548864 | bytes 16515685 | solution.py:30
  330.7 3.1 fusion.53
  333.8 3.7 fusion.54
  337.5 3.1 fusion.53
  340.7 3.7 fusion.54
  344.4 3.1 fusion.53
  347.5 3.7 fusion.54
  351.2 3.1 fusion.53
  354.4 3.7 fusion.54
  358.1 3.1 fusion.53
  361.2 3.7 fusion.54
  364.9 3.1 fusion.53
  368.1 3.7 fusion.54
  371.8 3.1 fusion.53
  374.9 3.7 fusion.54
  378.6 3.1 fusion.53
  381.8 3.7 fusion.54
  385.5 1.3 copy-done
  386.9 62.5 %reduce-scatter.5.cloned.1.call-done = f32[256,128]{1,0:T(8,128)} async-done(((f32[4096,128]{1,0:T(8,128)}), f32[256,128]{1,0:T(8,128)}) %reduce-scatter.5.cloned.1.call-update) | async-done | bytes 131088 | tf_op jit(solution)/shard_map/reduce_scatter | solution.py:43
  450.4 20.4 %all-reduce.2 = (f32[128]{0:T(128)S(1)}, f32[128]{0:T(128)S(1)}) all-reduce(f32[128]{0:T(128)S(1)} %get-tuple-element.59, f32[128]{0:T(128)S(1)} %get-tuple-element.58), channel_id=1, replica_groups=mesh['row'=8,'col'=16] {'row'}, use_global_device_ids=true, to_apply=%region_20.21 | all-reduce | flops 256 | bytes 2048 | tf_op jit(solution)/shard_map/psum | solution.py:12
  470.8 34.2 %all-reduce = (f32[128]{0:T(128)S(1)}, f32[128]{0:T(128)S(1)}) all-reduce(f32[128]{0:T(128)S(1)} %get-tuple-element.86, f32[128]{0:T(128)S(1)} %get-tuple-element.87), channel_id=1, replica_groups=mesh['row'=8,'col'=16] {'col'}, use_global_device_ids=true, to_apply=%region_21.22 | all-reduce | flops 256 | bytes 2048 | tf_op jit(solution)/shard_map/psum | solution.py:12
  (68 shorter events, 11.1 us)
Async XLA Ops:
  7.2 51.8 %all-gather.6.cloned.1.call-start = ((), (), s32[]{:S(2)}) async-start(), calls=%async_computation.3 | async-start | bytes 1179648 | tf_op jit(solution)/shard_map/all_gather | solution.py:42
  9.9 104.8 %all-gather.4.cloned.1.call-start = ((), (), s32[]{:S(2)}) async-start(), calls=%async_computation.2 | async-start | bytes 2359296 | tf_op jit(solution)/shard_map/all_gather | solution.py:37
  11.7 219.8 %reduce-scatter.3.cloned.1.call-start = ((), (), s32[]{:S(2)}) async-start(), calls=%async_computation.4 | async-start | bytes 2228224 | tf_op jit(solution)/shard_map/reduce_scatter | solution.py:43
  114.8 116.7 %copy-start.3 = (f32[256,128]{1,0:T(8,128)S(1)}, f32[256,128]{1,0:T(8,128)}, u32[]{:S(2)}) copy-start(f32[256,128]{1,0:T(8,128)} %param.7) | copy-start | bytes 393220
  114.8 3.1 copy-start.5
  121.7 3.1 copy-start.5
  128.6 3.1 copy-start.5
  135.4 3.1 copy-start.5
  142.3 3.1 copy-start.5
  149.1 3.1 copy-start.5
  156.0 3.1 copy-start.5
  162.8 3.1 copy-start.5
  169.7 1.3 copy-start.1
  171.0 159.5 %all-gather.8.cloned.1.call-start = ((), (), s32[]{:S(2)}) async-start(), calls=%async_computation.5 | async-start | bytes 1179648 | tf_op jit(solution)/shard_map/all_gather | solution.py:42
  292.2 157.2 %reduce-scatter.5.cloned.1.call-start = ((), (), s32[]{:S(2)}) async-start(), calls=%async_computation.6 | async-start | bytes 2228224 | tf_op jit(solution)/shard_map/reduce_scatter | solution.py:43
  330.6 118.7 %copy-start.2 = (f32[256,128]{1,0:T(8,128)S(1)}, f32[256,128]{1,0:T(8,128)}, u32[]{:S(2)}) copy-start(f32[256,128]{1,0:T(8,128)} %reduce-scatter.3.cloned.1.call-done) | copy-start | bytes 393220
  330.7 3.1 copy-start.6
  337.5 3.1 copy-start.6
  344.4 3.1 copy-start.6
  351.2 3.1 copy-start.6
  358.1 3.1 copy-start.6
  364.9 3.1 copy-start.6
  371.8 3.1 copy-start.6
  378.6 3.1 copy-start.6
  385.5 1.4 copy-start
  508.2 0.8 copy-start.4
Sparse Core Ops, SparseCore 0:
  10.9 48.0 all-gather.5
  61.3 53.3 all-gather.3
  171.1 60.3 reduce-scatter.2
  292.3 38.1 all-gather.7
  387.0 62.3 reduce-scatter.4
